TPU v7x, 32 devices: a whole 2x2x4 slice. The times are simulated.
32 devices in a mesh: dp: 8 (over z, x), mp: 4 (over y, core).
Axes of the slice: x: 2, y: 2, z: 4, core: 2. Of those that a mesh axis runs over, the one named last changes fastest.
Arguments:
- tokens: bfloat16 [24, 512, 768], P('dp'), may hold values from -6 to 6
- lengths: int32 [24], P('dp'), may hold values from 216 to 512, as said below
- gain_attn: bfloat16 [768], replicated, may hold values from 0.5 to 1.5
- bias_attn: bfloat16 [768], replicated, may hold values from -4 to 4
- query_w: bfloat16 [768, 768], P(None, 'mp'), may hold values from -0.21875 to 0.21875
- query_b: bfloat16 [768], P('mp'), may hold values from -4 to 4
- key_w: bfloat16 [768, 768], P(None, 'mp'), may hold values from -0.21875 to 0.21875
- value_w: bfloat16 [768, 768], P(None, 'mp'), may hold values from -0.21875 to 0.21875
- value_b: bfloat16 [768], P('mp'), may hold values from -0.75 to 0.75
- out_w: bfloat16 [768, 768], P('mp'), may hold values from -1.75 to 1.75
- out_b: bfloat16 [768], replicated, may hold values from -4 to 4
- gain_mlp: bfloat16 [768], replicated, may hold values from 0.5 to 1.5
- bias_mlp: bfloat16 [768], replicated, may hold values from -4 to 4
- up_w: bfloat16 [768, 3072], P(None, 'mp'), may hold values from -0.21875 to 0.21875
- up_b: bfloat16 [3072], P('mp'), may hold values from -4 to 4
- down_w: bfloat16 [3072, 768], P('mp'), may hold values from -0.15625 to 0.15625
- down_b: bfloat16 [768], replicated, may hold values from -4 to 4
- deconv_w: bfloat16 [768, 1024], P(None, 'mp'), may hold values from -0.21875 to 0.21875
- scale_norm: bfloat16 [128], replicated, may hold values from 0.5 to 1.5
- shift_norm: bfloat16 [128], replicated, may hold values from -6 to 6
- cotangent: bfloat16 [24, 512, 1024], P('dp', None, 'mp'), may hold values from -6 to 6
Outputs:
- volume: float32 [24, 512, 1024], P('dp', None, 'mp')
- grad_tokens: float32 [12288, 768], P(('dp', 'mp'))
- grad_gain_attn: float32 [768], replicated
- grad_bias_attn: float32 [768], replicated
- grad_query_w: float32 [768, 768], P(None, 'mp')
- grad_query_b: float32 [768], P('mp')
- grad_key_w: float32 [768, 768], P(None, 'mp')
- grad_value_w: float32 [768, 768], P(None, 'mp')
- grad_value_b: float32 [768], P('mp')
- grad_out_w: float32 [768, 768], P('mp')
- grad_out_b: float32 [768], replicated
- grad_gain_mlp: float32 [768], replicated
- grad_bias_mlp: float32 [768], replicated
- grad_up_w: float32 [768, 3072], P(None, 'mp')
- grad_up_b: float32 [3072], P('mp')
- grad_down_w: float32 [3072, 768], P('mp')
- grad_down_b: float32 [768], replicated
- grad_deconv_w: float32 [768, 1024], P(None, 'mp')
- grad_scale_norm: float32 [128], replicated
- grad_shift_norm: float32 [128], replicated
Inputs may be any that keep to these rules, and one draw needn't show every extreme that they name: `lengths`: each item holds 216, 256 or 512 patches, drawn independently for each item except that the first item of the whole batch holds 512.
All inputs are finite; a program needn't handle non-finite values.
Results may differ from a plain program's by a relative error of at most 0.025.
Values may be sent and summed in bfloat16 or wider, within the bound.
No kernel may reach another device: no remote copies, remote signals or barrier semaphores. Data moves between devices by JAX's collectives and lax.ppermute only.
A program may use at most 128 MiB of HBM per device.

v0:
```python
import jax
import jax.numpy as jnp
from jax import lax
from jax.sharding import PartitionSpec as P

HEAD_DIM = 64
CH = 128


EPSILON = 1e-05


def layer_norm(values, gain_vec, bias_vec):
    center = values - jnp.mean(values, axis=-1, keepdims=True)
    inverse = lax.rsqrt(jnp.mean(center * center, axis=-1, keepdims=True) + EPSILON)
    normal = center * inverse
    return (normal * gain_vec + bias_vec, normal, inverse)


def norm_backward(upstream, normal, inverse, gain_vec):
    scaled = upstream * gain_vec
    mean_part = jnp.mean(scaled, axis=-1, keepdims=True)
    mean_cross = jnp.mean(scaled * normal, axis=-1, keepdims=True)
    return inverse * (scaled - mean_part - normal * mean_cross)


def contract_rows(left_side, right_side):
    return lax.dot_general(
        left_side, right_side, (((0,), (0,)), ((), ())), preferred_element_type=jnp.float32
    )


def contract_cols(left_side, right_side):
    return lax.dot_general(
        left_side, right_side, (((1,), (1,)), ((), ())), preferred_element_type=jnp.float32
    )


def gelu_exact(values):
    return jax.nn.gelu(values, approximate=False)


def masked_scores(queries, key_rows, key_valid):
    scores = jnp.einsum(
        "qhe,khe->hqk", queries, key_rows, preferred_element_type=jnp.float32
    ) * HEAD_DIM ** (-0.5)
    return jnp.where(key_valid[None, None, :], scores, -1000000000.0)


def attention_forward(queries, key_rows, value_rows, key_valid):
    scores = masked_scores(queries, key_rows, key_valid)
    maximum = jnp.max(scores, axis=-1, keepdims=True)
    raised = jnp.exp(scores - maximum)
    summed = jnp.sum(raised, axis=-1, keepdims=True)
    probability = (raised / summed).astype(jnp.bfloat16)
    mixture = jnp.einsum(
        "hqk,khe->qhe", probability, value_rows, preferred_element_type=jnp.float32
    )
    return (mixture.astype(jnp.bfloat16), (maximum + jnp.log(summed))[..., 0])


def attention_backward(queries, key_rows, value_rows, key_valid, upstream, logsum):
    scores = masked_scores(queries, key_rows, key_valid)
    probability = jnp.exp(scores - logsum[..., None])
    value_grad = jnp.einsum(
        "hqk,qhe->khe",
        probability.astype(jnp.bfloat16),
        upstream,
        preferred_element_type=jnp.float32,
    )
    prob_grad = jnp.einsum("qhe,khe->hqk", upstream, value_rows, preferred_element_type=jnp.float32)
    row_term = jnp.sum(probability * prob_grad, axis=-1, keepdims=True)
    score_grad = (probability * (prob_grad - row_term)).astype(jnp.bfloat16)
    query_grad = jnp.einsum(
        "hqk,khe->qhe", score_grad, key_rows, preferred_element_type=jnp.float32
    ) * HEAD_DIM ** (-0.5)
    key_grad = jnp.einsum(
        "hqk,qhe->khe", score_grad, queries, preferred_element_type=jnp.float32
    ) * HEAD_DIM ** (-0.5)
    return (
        query_grad.astype(jnp.bfloat16),
        key_grad.astype(jnp.bfloat16),
        value_grad.astype(jnp.bfloat16),
    )


def shards(
    tokens,
    lengths,
    gain_attn,
    bias_attn,
    query_w,
    query_b,
    key_w,
    value_w,
    value_b,
    out_w,
    out_b,
    gain_mlp,
    bias_mlp,
    up_w,
    up_b,
    down_w,
    down_b,
    deconv_w,
    scale_norm,
    shift_norm,
    cotangent,
):
    item_count, seq_len, model_width = tokens.shape
    row_count = item_count * seq_len
    share_rows = row_count // lax.axis_size("mp")
    offset = lax.axis_index("mp") * share_rows
    residual = tokens.astype(jnp.float32).reshape(row_count, model_width)
    key_valid = jnp.arange(seq_len)[None, :] < lengths[:, None]
    rowmask = key_valid.astype(jnp.float32)[:, :, None, None]
    gain_one = gain_attn.astype(jnp.float32)
    gain_two = gain_mlp.astype(jnp.float32)
    scale_vec = scale_norm.astype(jnp.float32)
    normed, normal_one, inverse_one = layer_norm(residual, gain_one, bias_attn.astype(jnp.float32))
    normed = normed.astype(jnp.bfloat16)
    queries = (
        jnp.dot(normed, query_w, preferred_element_type=jnp.float32) + query_b.astype(jnp.float32)
    ).astype(jnp.bfloat16)
    key_rows = jnp.dot(normed, key_w, preferred_element_type=jnp.float32).astype(jnp.bfloat16)
    value_rows = (
        jnp.dot(normed, value_w, preferred_element_type=jnp.float32) + value_b.astype(jnp.float32)
    ).astype(jnp.bfloat16)
    local_heads = queries.shape[1] // HEAD_DIM
    head_shape = (item_count, seq_len, local_heads, HEAD_DIM)
    query_heads = queries.reshape(head_shape)
    key_heads = key_rows.reshape(head_shape)
    value_heads = value_rows.reshape(head_shape)

    def forward_item(inputs):
        item_query, item_keys, item_values, length = inputs
        item_valid = jnp.arange(seq_len) < length
        return attention_forward(item_query, item_keys, item_values, item_valid)

    mixture, logsums = lax.map(forward_item, (query_heads, key_heads, value_heads, lengths))
    mixture = mixture.reshape(row_count, local_heads * HEAD_DIM)
    attn_sum = lax.psum(
        jnp.dot(mixture, out_w, preferred_element_type=jnp.float32).astype(jnp.bfloat16), "mp"
    ).astype(jnp.float32)
    middle = residual + attn_sum + out_b.astype(jnp.float32)
    normed_two, normal_two, inverse_two = layer_norm(middle, gain_two, bias_mlp.astype(jnp.float32))
    normed_two = normed_two.astype(jnp.bfloat16)
    preact = jnp.dot(normed_two, up_w, preferred_element_type=jnp.float32) + up_b.astype(
        jnp.float32
    )
    active = gelu_exact(preact).astype(jnp.bfloat16)
    mlp_sum = lax.psum(
        jnp.dot(active, down_w, preferred_element_type=jnp.float32).astype(jnp.bfloat16), "mp"
    ).astype(jnp.float32)
    output_rows = middle + mlp_sum + down_b.astype(jnp.float32)
    output_low = output_rows.astype(jnp.bfloat16)
    normal_two_mine = lax.dynamic_slice_in_dim(normal_two, offset, share_rows, 0)
    inverse_two_mine = lax.dynamic_slice_in_dim(inverse_two, offset, share_rows, 0)
    deconv = jnp.dot(output_low, deconv_w, preferred_element_type=jnp.float32).reshape(
        item_count, seq_len, -1, CH
    )
    sum_values, sum_squares = lax.psum(
        (jnp.sum(deconv * rowmask, axis=(1, 2)), jnp.sum(deconv * deconv * rowmask, axis=(1, 2))),
        "mp",
    )
    voxels = (8 * lengths).astype(jnp.float32)[:, None]
    center = sum_values / voxels
    spread = lax.rsqrt(sum_squares / voxels - center * center + EPSILON)
    normal = (deconv - center[:, None, None, :]) * spread[:, None, None, :]
    volume = (rowmask * (scale_vec * normal + shift_norm.astype(jnp.float32))).reshape(
        item_count, seq_len, -1
    )
    upstream = cotangent.astype(jnp.float32).reshape(item_count, seq_len, -1, CH) * rowmask
    plain_sum, cross_sum = lax.psum(
        (jnp.sum(upstream, axis=(1, 2)), jnp.sum(upstream * normal, axis=(1, 2))), "mp"
    )
    scale_grad = jnp.sum(cross_sum, axis=0)
    shift_grad = jnp.sum(plain_sum, axis=0)
    voxel_grid = voxels[:, :, None, None]
    deconv_grad = (
        rowmask
        * spread[:, None, None, :]
        * scale_vec
        * (
            upstream
            - plain_sum[:, None, None, :] / voxel_grid
            - normal * cross_sum[:, None, None, :] / voxel_grid
        )
    )
    deconv_grad = deconv_grad.reshape(row_count, -1).astype(jnp.bfloat16)
    deconv_w_grad = contract_rows(output_low, deconv_grad)
    output_grad = lax.psum_scatter(
        contract_cols(deconv_grad, deconv_w).astype(jnp.bfloat16),
        "mp",
        scatter_dimension=0,
        tiled=True,
    ).astype(jnp.float32)
    down_upstream = lax.all_gather(output_grad.astype(jnp.bfloat16), "mp", axis=0, tiled=True)
    down_w_grad = contract_rows(active, down_upstream)
    active_grad = contract_cols(down_upstream, down_w)
    unused, gelu_back = jax.vjp(gelu_exact, preact)
    preact_grad = gelu_back(active_grad)[0].astype(jnp.bfloat16)
    up_w_grad = contract_rows(normed_two, preact_grad)
    up_b_grad = jnp.sum(preact_grad.astype(jnp.float32), axis=0)
    normed_two_grad = lax.psum_scatter(
        contract_cols(preact_grad, up_w).astype(jnp.bfloat16), "mp", scatter_dimension=0, tiled=True
    ).astype(jnp.float32)
    middle_grad = output_grad + norm_backward(
        normed_two_grad, normal_two_mine, inverse_two_mine, gain_two
    )
    gain_two_grad = jnp.sum(normed_two_grad * normal_two_mine, axis=0)
    bias_two_grad = jnp.sum(normed_two_grad, axis=0)
    down_b_grad = jnp.sum(output_grad, axis=0)
    out_b_grad = jnp.sum(middle_grad, axis=0)
    mixture_upstream = lax.all_gather(middle_grad.astype(jnp.bfloat16), "mp", axis=0, tiled=True)
    out_w_grad = contract_rows(mixture, mixture_upstream)
    mixture_grad = contract_cols(mixture_upstream, out_w).astype(jnp.bfloat16).reshape(head_shape)

    def backward_item(inputs):
        item_query, item_keys, item_values, length, item_upstream, logsum = inputs
        item_valid = jnp.arange(seq_len) < length
        return attention_backward(
            item_query, item_keys, item_values, item_valid, item_upstream, logsum
        )

    query_grad, key_grad, value_grad = lax.map(
        backward_item, (query_heads, key_heads, value_heads, lengths, mixture_grad, logsums)
    )
    query_grad = query_grad.reshape(row_count, -1)
    key_grad = key_grad.reshape(row_count, -1)
    value_grad = value_grad.reshape(row_count, -1)
    query_w_grad = contract_rows(normed, query_grad)
    query_b_grad = jnp.sum(query_grad.astype(jnp.float32), axis=0)
    key_w_grad = contract_rows(normed, key_grad)
    value_w_grad = contract_rows(normed, value_grad)
    value_b_grad = jnp.sum(value_grad.astype(jnp.float32), axis=0)
    normed_grad = lax.psum_scatter(
        (
            contract_cols(query_grad, query_w)
            + contract_cols(key_grad, key_w)
            + contract_cols(value_grad, value_w)
        ).astype(jnp.bfloat16),
        "mp",
        scatter_dimension=0,
        tiled=True,
    ).astype(jnp.float32)
    normal_one_mine = lax.dynamic_slice_in_dim(normal_one, offset, share_rows, 0)
    inverse_one_mine = lax.dynamic_slice_in_dim(inverse_one, offset, share_rows, 0)
    tokens_grad = middle_grad + norm_backward(
        normed_grad, normal_one_mine, inverse_one_mine, gain_one
    )
    gain_one_grad = jnp.sum(normed_grad * normal_one_mine, axis=0)
    bias_one_grad = jnp.sum(normed_grad, axis=0)
    stacked = jnp.stack(
        [gain_one_grad, bias_one_grad, gain_two_grad, bias_two_grad, out_b_grad, down_b_grad]
    )
    vectors = lax.psum(stacked, ("dp", "mp"))
    (
        query_w_grad,
        query_b_grad,
        key_w_grad,
        value_w_grad,
        value_b_grad,
        out_w_grad,
        up_w_grad,
        up_b_grad,
        down_w_grad,
        deconv_w_grad,
        scale_grad,
        shift_grad,
    ) = lax.psum(
        (
            query_w_grad,
            query_b_grad,
            key_w_grad,
            value_w_grad,
            value_b_grad,
            out_w_grad,
            up_w_grad,
            up_b_grad,
            down_w_grad,
            deconv_w_grad,
            scale_grad,
            shift_grad,
        ),
        "dp",
    )
    return (
        volume,
        tokens_grad,
        vectors[0],
        vectors[1],
        query_w_grad,
        query_b_grad,
        key_w_grad,
        value_w_grad,
        value_b_grad,
        out_w_grad,
        vectors[4],
        vectors[2],
        vectors[3],
        up_w_grad,
        up_b_grad,
        down_w_grad,
        vectors[5],
        deconv_w_grad,
        scale_grad,
        shift_grad,
    )


def solution(mesh):
    in_specs = (
        P("dp", None, None),
        P("dp"),
        P(),
        P(),
        P(None, "mp"),
        P("mp"),
        P(None, "mp"),
        P(None, "mp"),
        P("mp"),
        P("mp", None),
        P(),
        P(),
        P(),
        P(None, "mp"),
        P("mp"),
        P("mp", None),
        P(),
        P(None, "mp"),
        P(),
        P(),
        P("dp", None, "mp"),
    )
    out_specs = (
        P("dp", None, "mp"),
        P(("dp", "mp"), None),
        P(),
        P(),
        P(None, "mp"),
        P("mp"),
        P(None, "mp"),
        P(None, "mp"),
        P("mp"),
        P("mp", None),
        P(),
        P(),
        P(),
        P(None, "mp"),
        P("mp"),
        P("mp", None),
        P(),
        P(None, "mp"),
        P(),
        P(),
    )
    return jax.shard_map(shards, mesh=mesh, in_specs=in_specs, out_specs=out_specs, check_vma=False)
```

profile of v0, /device:TPU:0, one launch (start us, length us, event | category | flops | bytes accessed | tf_op | source)
XLA Modules:
  0.0 759.7 jit_solution(6580998958837947898)
XLA Ops:
  15.7 3.8 fusion.61
  26.8 3.4 fusion.70
  34.4 3.4 convolution_convert_fusion.5
  42.9 20.7 %while.26 = (s32[]{:T(128)}, bf16[3,512,3,64]{1,3,2,0:T(8,128)(2,1)}, f32[3,3,512]{2,1,0:T(4,128)}, bf16[3,512,3,64]{1,3,2,0:T(8,128)(2,1)}, s32[3]{0:T(128)S(1)...) while((s32[]{:T(128)}, bf16[3,512,3,64]{1,3,2,0:T(8,128)(2,1)}, ...), condition=%wide.region_5.6_spmd, body=%wide.region_2.5_spmd.sunk | while | flops 210861056 | bytes 10279525 | solution.py:140
  66.1 3.2 convolution_convert_fusion.3
  71.3 56.6 %all-reduce.8.cloned.1.call-done = bf16[1536,768]{1,0:T(8,128)(2,1)} async-done(((bf16[1536,768]{1,0:T(8,128)(2,1)}), bf16[1536,768]{1,0:T(8,128)(2,1)}) %all-reduce.8.cloned.1.call-update) | async-done | bytes 2359312 | tf_op jit(solution)/shard_map/psum | solution.py:142
  127.9 2.7 fusion.68
  132.8 13.2 %multiply_convert_fusion.1 = (bf16[1536,768]{1,0:T(8,128)(2,1)S(1)}, f32[1536,768]{1,0:T(8,128)}, f32[1536,768]{1,0:T(8,128)}) fusion(f32[768]{0:T(1024)S(1)} %convert_element_type.185, bf16[768,768]{1,0:T(8,128)(2,1)S(1)} %copy-done, f32[1536,768]{1,0:T(8,128)S(1)} %subtract_multiply_fusion, f32[768]{0:T(1024)S(1)} %convert_element_type.183, ...), kind=kOutput, calls=%fused_computation.78 | convolution fusion | flops 1893335040 | bytes 17703936 | tf_op jit(solution)/shard_map/dot_general | solution.py:148
  147.5 3.4 convolution_convert_fusion.2
  159.0 47.8 %all-reduce.10.cloned.1.call-done = bf16[1536,768]{1,0:T(8,128)(2,1)} async-done(((bf16[1536,768]{1,0:T(8,128)(2,1)}), bf16[1536,768]{1,0:T(8,128)(2,1)}) %all-reduce.10.cloned.1.call-update) | async-done | bytes 2359312 | tf_op jit(solution)/shard_map/psum | solution.py:152
  206.8 3.6 add_convert_fusion.2
  213.9 2.9 reshape.331
  216.8 4.7 multiply_reduce_fusion.4
  221.5 6.5 all-reduce.3
  230.6 3.9 multiply_reduce_fusion.5
  238.3 6.5 all-reduce.2
  252.4 34.0 %reduce-scatter.4.cloned.1.call-done = bf16[384,768]{1,0:T(8,128)(2,1)} async-done(((bf16[1536,768]{1,0:T(8,128)(2,1)}), bf16[384,768]{1,0:T(8,128)(2,1)}) %reduce-scatter.4.cloned.1.call-update) | async-done | bytes 589840 | tf_op jit(solution)/shard_map/reduce_scatter | solution.py:192
  286.4 25.5 %all-gather.3.cloned.1.call-done = bf16[1536,768]{1,0:T(8,128)(2,1)} async-done(((bf16[384,768]{1,0:T(8,128)(2,1)}), bf16[1536,768]{1,0:T(8,128)(2,1)}) %all-gather.3.cloned.1.call-update) | async-done | bytes 2359312 | tf_op jit(solution)/shard_map/all_gather | solution.py:198
  312.0 8.8 %convert_reduce_fusion.1 = (f32[768]{0:T(1024)}, bf16[1536,768]{1,0:T(8,128)(2,1)S(1)}) fusion(f32[1536,768]{1,0:T(8,128)} %get-tuple-element.241, f32[1536,768]{1,0:T(8,128)} %get-tuple-element.256, f32[768]{0:T(1024)S(1)} %copy-done.63, bf16[1536,768]{1,0:T(8,128)(2,1)} %all-gather.3.cloned.1.call-done, bf16[768,768]{1,0:T(8,128)(2,1)} %param.40), kind=kOutput, calls=%fused_computation.74 | convolution fusion | flops 1831992576 | bytes 15341568 | tf_op jit(solution)/shard_map/dot_general | solution.py:34
  322.1 3.5 convolution_convert_fusion
  326.5 32.4 %reduce-scatter.6.cloned.1.call-done = bf16[384,768]{1,0:T(8,128)(2,1)} async-done(((bf16[1536,768]{1,0:T(8,128)(2,1)}), bf16[384,768]{1,0:T(8,128)(2,1)}) %reduce-scatter.6.cloned.1.call-update) | async-done | bytes 589840 | tf_op jit(solution)/shard_map/reduce_scatter | solution.py:205
  361.3 2.6 fusion.94
  366.2 24.0 %all-gather.5.cloned.1.call-done = bf16[1536,768]{1,0:T(8,128)(2,1)} async-done(((bf16[384,768]{1,0:T(8,128)(2,1)}), bf16[1536,768]{1,0:T(8,128)(2,1)}) %all-gather.5.cloned.1.call-update) | async-done | bytes 2359312 | tf_op jit(solution)/shard_map/all_gather | solution.py:215
  390.1 3.4 convolution_convert_fusion.4
  400.4 30.7 %while.27 = (s32[]{:T(128)}, bf16[3,512,3,64]{1,3,2,0:T(8,128)(2,1)}, bf16[3,512,3,64]{1,3,2,0:T(8,128)(2,1)}, bf16[3,512,3,64]{1,3,2,0:T(8,128)(2,1)}, bf16[3,5...) while((s32[]{:T(128)}, ...), condition=%wide.region_26.27_spmd, body=%wide.region_24.26_spmd.sunk | while | flops 510884864 | bytes 30316728 | solution.py:226
  442.2 3.0 fusion.102
  445.2 5.4 fusion.101
  450.6 3.5 fusion.90
  462.7 22.2 %all-reduce = (f32[192]{0:T(256)}, f32[192]{0:T(256)}, f32[768]{0:T(1024)}, f32[128]{0:T(128)}, f32[128]{0:T(128)}) all-reduce(f32[192]{0:T(256)S(1)} %reduce_sum.266, f32[192]{0:T(256)S(1)} %reduce_sum.268, f32[768]{0:T(1024)S(1)} %copy-done.59, f32[128]{0:T(128)S(1)} %reduce_sum.270, ...), channel_id=1, replica_groups=mesh['dp'=8,'mp'=4] {'dp'}, use_global_device_ids=true, to_apply=%region_39.40 | all-reduce | flops 1408 | bytes 11264 | tf_op jit(solution)/shard_map/psum | solution.py:271
  486.9 42.7 %psum.139 = f32[6,768]{1,0:T(8,128)S(1)} all-reduce(f32[6,768]{1,0:T(8,128)S(1)} %stack.27), channel_id=1, replica_groups=mesh['dp'=8,'mp'=4] {'dp','mp'}, use_global_device_ids=true, to_apply=%region_36.37 | all-reduce | flops 4608 | bytes 36864 | tf_op jit(solution)/shard_map/psum | solution.py:257
  530.2 2.8 fusion.83
  533.0 208.7 %all-reduce.12.cloned.1.call-done = (f32[768,192]{0,1:T(8,128)}, f32[768,192]{0,1:T(8,128)}, f32[768,192]{0,1:T(8,128)}, f32[192,768]{1,0:T(8,128)}, f32[768,768...) async-done(((f32[768,192]{0,1:T(8,128)}, f32[768,192]{0,1:T(8,128)}, f32[768,192]{0,1:T(8,128)}, f32[192,768]{1,0:T(8,128)}, f32[768,768]{1,0:T(8,128)}, ...) | async-done | bytes 7864336 | tf_op jit(solution)/shard_map/psum | solution.py:271
  (332 shorter events, 156.0 us)
Async XLA Ops:
  7.2 125.6 %copy-start = (bf16[768,768]{1,0:T(8,128)(2,1)S(1)}, bf16[768,768]{1,0:T(8,128)(2,1)}, u32[]{:S(2)}) copy-start(bf16[768,768]{1,0:T(8,128)(2,1)} %param.38) | copy-start | bytes 3538948
  7.2 120.7 %all-reduce.8.cloned.1.call-start = ((), (), s32[]{:S(2)}) async-start(), calls=%async_computation.3 | async-start | bytes 4718592 | tf_op jit(solution)/shard_map/psum | solution.py:142
  9.7 9.8 %copy-start.37 = (f32[3,512]{1,0:T(4,128)}, f32[3,512]{1,0:T(4,128)S(1)}, u32[]{:S(2)}) copy-start(f32[3,512]{1,0:T(4,128)S(1)} %broadcast_multiply_fusion.1) | copy-start | bytes 18436
  13.0 6.5 copy-start.41
  14.3 5.2 copy-start.39
  15.7 5.2 copy-start.35
  20.9 5.9 copy-start.72
  37.8 5.1 copy-start.68
  69.4 137.4 %all-reduce.10.cloned.1.call-start = ((), (), s32[]{:S(2)}) async-start(), calls=%async_computation.4 | async-start | bytes 4718592 | tf_op jit(solution)/shard_map/psum | solution.py:152
  69.9 291.4 %copy-start.45 = (f32[768]{0:T(1024)}, f32[768]{0:T(1024)S(1)}, u32[]{:S(2)}) copy-start(f32[768]{0:T(1024)S(1)} %convert_element_type.182) | copy-start | bytes 9220
  70.6 62.2 %copy-start.60 = (f32[768]{0:T(1024)}, f32[768]{0:T(1024)S(1)}, u32[]{:S(2)}) copy-start(f32[768]{0:T(1024)S(1)} %convert_element_type.183) | copy-start | bytes 9220
  71.3 61.5 %copy-start.62 = (f32[768]{0:T(1024)}, f32[768]{0:T(1024)S(1)}, u32[]{:S(2)}) copy-start(f32[768]{0:T(1024)S(1)} %convert_element_type.185) | copy-start | bytes 9220
  132.8 13.2 %copy-start.8 = (f32[1536,768]{1,0:T(8,128)}, f32[1536,768]{1,0:T(8,128)S(1)}, u32[]{:S(2)}) copy-start(f32[1536,768]{1,0:T(8,128)S(1)} %subtract_multiply_fusion) | copy-start | bytes 14155780
  132.8 14.6 %copy-start.71 = (bf16[768,768]{1,0:T(8,128)(2,1)S(1)}, bf16[768,768]{1,0:T(8,128)(2,1)}, u32[]{:S(2)}) copy-start(bf16[768,768]{1,0:T(8,128)(2,1)} %param.40) | copy-start | bytes 3538948
  150.9 135.5 %reduce-scatter.4.cloned.1.call-start = ((), (), s32[]{:S(2)}) async-start(), calls=%async_computation.5 | async-start | bytes 2949120 | tf_op jit(solution)/shard_map/reduce_scatter | solution.py:192
  206.8 5.1 copy-start.29
  234.5 13.2 %copy-start.51 = (f32[3,128]{1,0:T(4,128)S(1)}, f32[3,128]{1,0:T(4,128)}, u32[]{:S(2)}) copy-start(f32[3,128]{1,0:T(4,128)} %copy-done.50) | copy-start | bytes 4612
  250.1 61.9 %copy-start.63 = (f32[768]{0:T(1024)S(1)}, f32[768]{0:T(1024)}, u32[]{:S(2)}) copy-start(f32[768]{0:T(1024)} %copy-done.62) | copy-start | bytes 9220
  252.4 59.6 %all-gather.3.cloned.1.call-start = ((), (), s32[]{:S(2)}) async-start(), calls=%async_computation.6 | async-start | bytes 2949120 | tf_op jit(solution)/shard_map/all_gather | solution.py:198
  286.4 72.5 %reduce-scatter.6.cloned.1.call-start = ((), (), s32[]{:S(2)}) async-start(), calls=%async_computation.7 | async-start | bytes 2949120 | tf_op jit(solution)/shard_map/reduce_scatter | solution.py:205
  325.6 64.5 %all-gather.5.cloned.1.call-start = ((), (), s32[]{:S(2)}) async-start(), calls=%async_computation.8 | async-start | bytes 2949120 | tf_op jit(solution)/shard_map/all_gather | solution.py:215
  365.9 119.0 %reduce-scatter.8.cloned.1.call-start = ((), (), s32[]{:S(2)}) async-start(), calls=%async_computation.9 | async-start | bytes 2949120 | tf_op jit(solution)/shard_map/reduce_scatter | solution.py:237
  393.5 6.8 copy-start.69
  439.9 301.8 %all-reduce.12.cloned.1.call-start = ((), (), s32[]{:S(2)}) async-start(), calls=%async_computation.10 | async-start | bytes 15728640 | tf_op jit(solution)/shard_map/psum | solution.py:271
  440.3 10.3 %slice-start = ((s8[4718592]{0:T(1024)(128)(4,1)}), s8[4194304]{0:T(1024)(128)(4,1)S(1)}, s32[]{:S(2)}) async-start(s8[4718592]{0:T(1024)(128)(4,1)} %bitcast.262), calls=%async_computation.11 | async-start | bytes 8388608
  442.2 8.4 %slice-start.1 = ((s8[4718592]{0:T(1024)(128)(4,1)}), s8[524288]{0:T(1024)(128)(4,1)S(1)}, s32[]{:S(2)}) async-start(s8[4718592]{0:T(1024)(128)(4,1)} %bitcast.262), calls=%async_computation.12 | async-start | bytes 1048576
  445.1 5.4 copy-start.46
  445.2 5.4 copy-start.61
  445.2 5.4 copy-start.75
  460.1 70.1 %copy-start.10 = (f32[384,768]{1,0:T(8,128)S(1)}, f32[384,768]{1,0:T(8,128)}, u32[]{:S(2)}) copy-start(f32[384,768]{1,0:T(8,128)} %copy-done.9) | copy-start | bytes 3538948
  741.7 5.9 copy-start.32
  741.7 6.7 copy-start.24
  (58 other events, 129.7 us)
Sparse Core Ops, SparseCore 0:
  69.5 58.3 all-reduce.7
  151.0 55.7 all-reduce.9
  252.5 33.8 reduce-scatter.3
  287.9 24.0 all-gather.2
  325.8 33.0 reduce-scatter.5
  366.0 24.0 all-gather.4
  440.0 33.0 reduce-scatter.7
  481.2 260.4 all-reduce.11
where the time goes:
time: 768 us; the launch traced here: 760 us
  waiting for transfers between devices  429 us (56%)
  matrix products  105 us (14%)
  blocking collectives  77.8 us (10%)
  local copies, waits for them, and re-layouts  67.3 us (9%)
  other arithmetic  63.6 us (8%)
  between operations  15.4 us (2%)
    psum x1, waiting for transfers between devices, shards(): lax.psum((query_w_grad, query_b_grad, key_w_grad, value_w_grad, value_b_g...  209 us
    psum x1, waiting for transfers between devices, shards(): lax.psum(jnp.dot(mixture, out_w, preferred_element_type=jnp.float32).asty...  56.6 us
    psum x1, waiting for transfers between devices, shards(): lax.psum(jnp.dot(active, down_w, preferred_element_type=jnp.float32).asty...  47.8 us
    psum x1, blocking collectives, shards(): vectors = lax.psum(stacked, ('dp', 'mp'))  42.7 us
    reduce_scatter x1, waiting for transfers between devices, shards(): lax.psum_scatter(contract_cols(deconv_grad, deconv_w).astype(jnp.bfloat16...  34 us
    reduce_scatter x1, waiting for transfers between devices, shards(): lax.psum_scatter(contract_cols(preact_grad, up_w).astype(jnp.bfloat16), '...  32.4 us
    all_gather x1, waiting for transfers between devices, shards(): lax.all_gather(output_grad.astype(jnp.bfloat16), 'mp', axis=0, tiled=True)  25.5 us
    all_gather x1, waiting for transfers between devices, shards(): lax.all_gather(middle_grad.astype(jnp.bfloat16), 'mp', axis=0, tiled=True)  24 us
  transfers between devices with their start and end apart: 8, of which 7 were waited for; matrix products, arithmetic and copies ran while one was open for 5% of the time, Pallas kernels for 0%

commit v1 on v0

v1 whole, which is shorter than its diff:
```python
import functools

import jax
import jax.numpy as jnp
from jax import lax
from jax.experimental import pallas as pl
from jax.experimental.pallas import tpu as pltpu
from jax.sharding import PartitionSpec as P

HEAD_DIM = 64
CH = 128
EPSILON = 1e-05
SCALE = HEAD_DIM ** (-0.5)
F32 = jnp.float32
BF16 = jnp.bfloat16


def dot(left, right):
    return jnp.dot(left, right, preferred_element_type=F32)


def dot_rows(left, right):
    return lax.dot_general(left, right, (((0,), (0,)), ((), ())), preferred_element_type=F32)


def dot_cols(left, right):
    return lax.dot_general(left, right, (((1,), (1,)), ((), ())), preferred_element_type=F32)


def swap(value, axis, bit):
    size = lax.axis_size(axis)
    return lax.ppermute(value, axis, [(i, i ^ bit) for i in range(size)])


def norm_stats(values):
    center = values - jnp.mean(values, axis=-1, keepdims=True)
    inverse = lax.rsqrt(jnp.mean(center * center, axis=-1, keepdims=True) + EPSILON)
    return center * inverse, inverse


def norm_backward(upstream, normal, inverse, gain_vec):
    scaled = upstream * gain_vec
    mean_part = jnp.mean(scaled, axis=-1, keepdims=True)
    mean_cross = jnp.mean(scaled * normal, axis=-1, keepdims=True)
    return inverse * (scaled - mean_part - normal * mean_cross)


def head_cols(index, head, heads):
    start = (index * heads + head) * HEAD_DIM
    return slice(start, start + HEAD_DIM)


def attend_kernel(heads, seq, len_ref, qkv_ref, o_ref, lse_ref):
    length = len_ref[pl.program_id(0)]

    def run(span):
        valid = lax.broadcasted_iota(jnp.int32, (span, span), 0) < length
        for head in range(heads):
            query = qkv_ref[:span, head_cols(0, head, heads)] * jnp.asarray(SCALE, BF16)
            keys = qkv_ref[:span, head_cols(1, head, heads)]
            vals = qkv_ref[:span, head_cols(2, head, heads)]
            scores = jnp.where(valid, dot_cols(keys, query), -1e9)
            top = jnp.max(scores, axis=0, keepdims=True)
            raised = jnp.exp(scores - top)
            total = jnp.sum(raised, axis=0, keepdims=True)
            mixed = dot_rows(vals, raised.astype(BF16)) / total
            o_ref[:span, head_cols(0, head, heads)] = mixed.T.astype(BF16)
            lse_ref[0, head : head + 1, :span] = top + jnp.log(total)
        if span < seq:
            o_ref[span:, :] = jnp.zeros((seq - span, heads * HEAD_DIM), BF16)

    half = seq // 2

    @pl.when(length <= half)
    def _():
        run(half)

    @pl.when(length > half)
    def _():
        run(seq)


def attend(lengths, qkv, items, seq, heads):
    width = heads * HEAD_DIM
    flops = 4 * items * heads * seq * seq * HEAD_DIM
    return pl.pallas_call(
        functools.partial(attend_kernel, heads, seq),
        out_shape=(
            jax.ShapeDtypeStruct((items * seq, width), BF16),
            jax.ShapeDtypeStruct((items, 8, seq), F32),
        ),
        grid_spec=pltpu.PrefetchScalarGridSpec(
            num_scalar_prefetch=1,
            grid=(items,),
            in_specs=[pl.BlockSpec((seq, 3 * width), lambda i, n: (i, 0))],
            out_specs=(
                pl.BlockSpec((seq, width), lambda i, n: (i, 0)),
                pl.BlockSpec((1, 8, seq), lambda i, n: (i, 0, 0)),
            ),
        ),
        cost_estimate=pl.CostEstimate(
            flops=flops, transcendentals=items * heads * seq * seq, bytes_accessed=8 * items * seq * width
        ),
        name="attend",
    )(lengths, qkv)


def attend_back_kernel(heads, seq, len_ref, qkv_ref, do_ref, lse_ref, out_ref):
    length = len_ref[pl.program_id(0)]

    def run(span):
        valid = lax.broadcasted_iota(jnp.int32, (span, span), 0) < length
        for head in range(heads):
            query = qkv_ref[:span, head_cols(0, head, heads)] * jnp.asarray(SCALE, BF16)
            keys = qkv_ref[:span, head_cols(1, head, heads)]
            vals = qkv_ref[:span, head_cols(2, head, heads)]
            upstream = do_ref[:span, head_cols(0, head, heads)]
            scores = jnp.where(valid, dot_cols(keys, query), -1e9)
            prob = jnp.exp(scores - lse_ref[0, head : head + 1, :span])
            val_grad = dot(prob.astype(BF16), upstream)
            prob_grad = dot_cols(vals, upstream)
            product = prob * prob_grad
            row_term = jnp.sum(product, axis=0, keepdims=True)
            score_grad = (product - prob * row_term).astype(BF16)
            key_grad = dot(score_grad, query)
            query_grad = dot_rows(keys, score_grad) * SCALE
            out_ref[:span, head_cols(0, head, heads)] = query_grad.T.astype(BF16)
            out_ref[:span, head_cols(1, head, heads)] = key_grad.astype(BF16)
            out_ref[:span, head_cols(2, head, heads)] = val_grad.astype(BF16)
        if span < seq:
            out_ref[span:, :] = jnp.zeros((seq - span, 3 * heads * HEAD_DIM), BF16)

    half = seq // 2

    @pl.when(length <= half)
    def _():
        run(half)

    @pl.when(length > half)
    def _():
        run(seq)


def attend_back(lengths, qkv, upstream, logsum, items, seq, heads):
    width = heads * HEAD_DIM
    flops = 10 * items * heads * seq * seq * HEAD_DIM
    return pl.pallas_call(
        functools.partial(attend_back_kernel, heads, seq),
        out_shape=jax.ShapeDtypeStruct((items * seq, 3 * width), BF16),
        grid_spec=pltpu.PrefetchScalarGridSpec(
            num_scalar_prefetch=1,
            grid=(items,),
            in_specs=[
                pl.BlockSpec((seq, 3 * width), lambda i, n: (i, 0)),
                pl.BlockSpec((seq, width), lambda i, n: (i, 0)),
                pl.BlockSpec((1, 8, seq), lambda i, n: (i, 0, 0)),
            ],
            out_specs=pl.BlockSpec((seq, 3 * width), lambda i, n: (i, 0)),
        ),
        cost_estimate=pl.CostEstimate(
            flops=flops, transcendentals=items * heads * seq * seq, bytes_accessed=14 * items * seq * width
        ),
        name="attend_back",
    )(lengths, qkv, upstream, logsum)


def gather_mp(block):
    core = swap(block, "mp", 1)
    far = swap(block, "mp", 2)
    return [block, core, far, swap(far, "mp", 1)]


def exchange_mp(blocks):
    return [blocks[0]] + [swap(blocks[k], "mp", k) for k in (1, 2, 3)]


def scatter_sum_mp(blocks):
    first = swap(blocks[1].astype(BF16), "mp", 1)
    third = swap(blocks[3].astype(BF16), "mp", 1)
    passed = (blocks[2] + third.astype(F32)).astype(BF16)
    return blocks[0] + first.astype(F32) + swap(passed, "mp", 2).astype(F32)


def sum_dp(value):
    size = lax.axis_size("dp")
    index = lax.axis_index("dp")
    bits = []
    bit = 1
    while bit < size:
        bits.append(bit)
        bit *= 2
    current = value.astype(BF16)
    for bit in bits:
        half = current.shape[0] // 2
        high = (index & bit) > 0
        low_part, high_part = current[:half], current[half:]
        sent = jnp.where(high, low_part, high_part)
        kept = jnp.where(high, high_part, low_part)
        current = (kept.astype(F32) + swap(sent, "dp", bit).astype(F32)).astype(BF16)
    for bit in reversed(bits):
        high = (index & bit) > 0
        other = swap(current, "dp", bit)
        current = jnp.concatenate([jnp.where(high, other, current), jnp.where(high, current, other)], axis=0)
    return current.astype(F32)


def shards(
    tokens,
    lengths,
    gain_attn,
    bias_attn,
    query_w,
    query_b,
    key_w,
    value_w,
    value_b,
    out_w,
    out_b,
    gain_mlp,
    bias_mlp,
    up_w,
    up_b,
    down_w,
    down_b,
    deconv_w,
    scale_norm,
    shift_norm,
    cotangent,
):
    items, seq, width = tokens.shape
    rows = items * seq
    ways = lax.axis_size("mp")
    me = lax.axis_index("mp")
    share = rows // ways
    offset = me * share
    head_width = query_w.shape[1]
    heads = head_width // HEAD_DIM
    gain_one = gain_attn.astype(F32)
    gain_two = gain_mlp.astype(F32)
    scale_vec = scale_norm.astype(F32)

    def row_block(value, k):
        return lax.dynamic_slice_in_dim(value, (me ^ k) * share, share, 0)

    def place_rows(blocks, dtype):
        result = jnp.zeros((rows, blocks[0].shape[1]), dtype)
        for k in range(ways):
            result = lax.dynamic_update_slice_in_dim(result, blocks[k].astype(dtype), (me ^ k) * share, 0)
        return result

    out_full = jnp.concatenate(gather_mp(out_w), axis=0)
    up_blocks = gather_mp(up_w)
    up_bias = gather_mp(up_b.reshape(1, -1))
    down_blocks = gather_mp(down_w)
    deconv_full = jnp.concatenate(gather_mp(deconv_w), axis=1)
    cot_rows = cotangent.reshape(rows, -1)
    cot = jnp.concatenate(exchange_mp([row_block(cot_rows, k) for k in range(ways)]), axis=1)

    residual = tokens.reshape(rows, width).astype(F32)
    normal_one, inverse_one = norm_stats(residual)
    normed = (normal_one * gain_one + bias_attn.astype(F32)).astype(BF16)
    qkv_w = jnp.concatenate([query_w, key_w, value_w], axis=1)
    qkv_b = jnp.concatenate([query_b, jnp.zeros_like(query_b), value_b]).astype(F32)
    qkv = (dot(normed, qkv_w) + qkv_b).astype(BF16)
    mixture_heads, logsum = attend(lengths, qkv, items, seq, heads)
    mixture = jnp.concatenate(exchange_mp([row_block(mixture_heads, k) for k in range(ways)]), axis=1)

    my_tokens = lax.dynamic_slice_in_dim(tokens.reshape(rows, width), offset, share, 0).astype(F32)
    middle = my_tokens + dot(mixture, out_full) + out_b.astype(F32)
    normal_two, inverse_two = norm_stats(middle)
    normed_two = (normal_two * gain_two + bias_mlp.astype(F32)).astype(BF16)
    preacts = [dot(normed_two, up_blocks[k]) + up_bias[k].astype(F32) for k in range(ways)]
    actives = [jax.nn.gelu(u, approximate=False).astype(BF16) for u in preacts]
    output_rows = middle + down_b.astype(F32)
    for k in range(ways):
        output_rows = output_rows + dot(actives[k], down_blocks[k])
    output_low = output_rows.astype(BF16)
    deconv = dot(output_low, deconv_full)

    piece = share
    while seq % piece:
        piece //= 2 if piece % 2 == 0 else piece
    pieces = share // piece
    first_piece = me * pieces
    piece_start = (first_piece + jnp.arange(pieces)) * piece
    piece_item = piece_start // seq
    chosen = (piece_item[:, None] == jnp.arange(items)[None, :]).astype(F32)
    slot = (piece_start % seq)[:, None] + jnp.arange(piece)[None, :]
    piece_len = jnp.sum(chosen * lengths.astype(F32)[None, :], axis=1)
    rowmask = (slot.astype(F32) < piece_len[:, None]).astype(F32)[:, :, None, None]
    shape4 = (pieces, piece, -1, CH)
    deconv4 = deconv.reshape(shape4)
    upstream = cot.astype(F32).reshape(shape4) * rowmask
    masked = deconv4 * rowmask
    sums = jnp.stack(
        [
            jnp.sum(masked, axis=(1, 2)),
            jnp.sum(masked * deconv4, axis=(1, 2)),
            jnp.sum(upstream, axis=(1, 2)),
            jnp.sum(upstream * deconv4, axis=(1, 2)),
        ],
        axis=1,
    )
    sums = jnp.sum(chosen[:, :, None, None] * sums[:, None], axis=0).reshape(-1, CH)
    sums = sums + swap(sums, "mp", 1)
    sums = (sums + swap(sums, "mp", 2)).reshape(items, 4, CH)
    voxels = (8 * lengths).astype(F32)[:, None]
    center = sums[:, 0] / voxels
    spread = lax.rsqrt(sums[:, 1] / voxels - center * center + EPSILON)
    plain_sum = sums[:, 2]
    cross_sum = spread * (sums[:, 3] - center * plain_sum)
    scale_grad = jnp.sum(cross_sum, axis=0)
    shift_grad = jnp.sum(plain_sum, axis=0)

    def per_piece(values):
        return jnp.sum(chosen[:, :, None] * values[None], axis=1)[:, None, None, :]

    center_p = per_piece(center)
    spread_p = per_piece(spread)
    normal = (deconv4 - center_p) * spread_p
    volume_rows = (rowmask * (scale_vec * normal + shift_norm.astype(F32))).reshape(share, -1)
    deconv_grad = (
        rowmask
        * (spread_p * scale_vec)
        * (upstream - per_piece(plain_sum / voxels) - normal * per_piece(cross_sum / voxels))
    )
    deconv_grad = deconv_grad.reshape(share, -1).astype(BF16)
    block = volume_rows.shape[1] // ways
    volume_blocks = [volume_rows[:, k * block : (k + 1) * block].astype(BF16) for k in range(ways)]
    volume = place_rows(exchange_mp(volume_blocks), F32).reshape(items, seq, -1)

    output_grad = dot_cols(deconv_grad, deconv_full)
    output_grad_low = output_grad.astype(BF16)
    deconv_w_full = dot_rows(output_low, deconv_grad)
    deconv_w_grad = sum_dp(scatter_sum_mp([deconv_w_full[:, k * block : (k + 1) * block] for k in range(ways)]))
    normed_two_grad = jnp.zeros((share, width), F32)
    preact_grads = []
    for k in range(ways):
        active_grad = dot_cols(output_grad_low, down_blocks[k])
        unused, gelu_back = jax.vjp(lambda u: jax.nn.gelu(u, approximate=False), preacts[k])
        preact_grad = gelu_back(active_grad)[0].astype(BF16)
        preact_grads.append(preact_grad)
        normed_two_grad = normed_two_grad + dot_cols(preact_grad, up_blocks[k])
    down_w_grad = sum_dp(scatter_sum_mp([dot_rows(actives[k], output_grad_low) for k in range(ways)]))
    middle_grad = output_grad + norm_backward(normed_two_grad, normal_two, inverse_two, gain_two)
    middle_grad_low = middle_grad.astype(BF16)
    mixture_grad = dot_cols(middle_grad_low, out_full).astype(BF16)
    mixture_grad = place_rows(
        exchange_mp([mixture_grad[:, k * head_width : (k + 1) * head_width] for k in range(ways)]), BF16
    )
    up_w_grad = sum_dp(scatter_sum_mp([dot_rows(normed_two, preact_grads[k]) for k in range(ways)]))
    out_w_full = dot_rows(mixture, middle_grad_low)
    out_w_grad = sum_dp(scatter_sum_mp([out_w_full[k * head_width : (k + 1) * head_width] for k in range(ways)]))

    qkv_grad = attend_back(lengths, qkv, mixture_grad, logsum, items, seq, heads)
    qkv_w_grad = sum_dp(dot_rows(normed, qkv_grad))
    qkv_b_grad = jnp.sum(qkv_grad.astype(F32), axis=0)
    normed_part = dot_cols(qkv_grad, qkv_w)
    gain_one_grad = jnp.sum(normed_part * normal_one, axis=0)
    bias_one_grad = jnp.sum(normed_part, axis=0)
    normed_grad = scatter_sum_mp([row_block(normed_part, k) for k in range(ways)])
    my_normal, my_inverse = norm_stats(my_tokens)
    tokens_grad = middle_grad + norm_backward(normed_grad, my_normal, my_inverse, gain_one)

    up_b_parts = [jnp.sum(g.astype(F32), axis=0) for g in preact_grads]
    whole = jnp.stack(
        [
            gain_one_grad,
            bias_one_grad,
            jnp.sum(normed_two_grad * normal_two, axis=0),
            jnp.sum(normed_two_grad, axis=0),
            jnp.sum(middle_grad, axis=0),
            jnp.sum(output_grad, axis=0),
        ]
    )
    count = whole.shape[0]
    core = swap(jnp.concatenate([whole, up_b_parts[1][None], up_b_parts[3][None]], axis=0), "mp", 1)
    whole = whole + core[:count]
    far = swap(jnp.concatenate([whole, (up_b_parts[2] + core[count + 1])[None]], axis=0), "mp", 2)
    whole = whole + far[:count]
    up_b_grad = up_b_parts[0] + core[count] + far[count]
    flat = jnp.concatenate([whole.reshape(-1), up_b_grad, qkv_b_grad, scale_grad, shift_grad])
    lines = -(-flat.shape[0] // 1024) * 8
    flat = jnp.pad(flat, (0, lines * 128 - flat.shape[0])).reshape(lines, 128)
    bit = 1
    while bit < lax.axis_size("dp"):
        flat = flat + swap(flat, "dp", bit)
        bit *= 2
    flat = flat.reshape(-1)
    vectors = flat[: count * width].reshape(count, width)
    place = count * width
    up_b_grad = flat[place : place + up_b_grad.shape[0]]
    place += up_b_grad.shape[0]
    query_b_grad = flat[place : place + head_width]
    value_b_grad = flat[place + 2 * head_width : place + 3 * head_width]
    place += 3 * head_width
    scale_grad = flat[place : place + CH]
    shift_grad = flat[place + CH : place + 2 * CH]
    return (
        volume,
        tokens_grad,
        vectors[0],
        vectors[1],
        qkv_w_grad[:, :head_width],
        query_b_grad,
        qkv_w_grad[:, head_width : 2 * head_width],
        qkv_w_grad[:, 2 * head_width :],
        value_b_grad,
        out_w_grad,
        vectors[4],
        vectors[2],
        vectors[3],
        up_w_grad,
        up_b_grad,
        down_w_grad,
        vectors[5],
        deconv_w_grad,
        scale_grad,
        shift_grad,
    )


def solution(mesh):
    in_specs = (
        P("dp", None, None),
        P("dp"),
        P(),
        P(),
        P(None, "mp"),
        P("mp"),
        P(None, "mp"),
        P(None, "mp"),
        P("mp"),
        P("mp", None),
        P(),
        P(),
        P(),
        P(None, "mp"),
        P("mp"),
        P("mp", None),
        P(),
        P(None, "mp"),
        P(),
        P(),
        P("dp", None, "mp"),
    )
    out_specs = (
        P("dp", None, "mp"),
        P(("dp", "mp"), None),
        P(),
        P(),
        P(None, "mp"),
        P("mp"),
        P(None, "mp"),
        P(None, "mp"),
        P("mp"),
        P("mp", None),
        P(),
        P(),
        P(),
        P(None, "mp"),
        P("mp"),
        P("mp", None),
        P(),
        P(None, "mp"),
        P(),
        P(),
    )
    return jax.shard_map(shards, mesh=mesh, in_specs=in_specs, out_specs=out_specs, check_vma=False)
```

time: 768 us -> 514 us (0.67)
  waiting for transfers between devices: 429 us -> 260 us
  blocking collectives: 77.8 us -> 0 us
  starting transfers between devices: 1.25 us -> 58.9 us
  matrix products: 105 us -> 65.1 us
  local copies, waits for them, and re-layouts: 67.3 us -> 47.9 us
  Pallas kernels: 0 us -> 16.9 us
  between operations: 15.4 us -> 2.9 us
  other arithmetic: 63.6 us -> 52.7 us
    psum x3 -> x0, waiting for transfers between devices: 313 us -> none  [the longest x1 209 us: shards(): lax.psum((query_w_grad, query_b_grad, key_w_grad, value_w_grad, value_b_g...]
    ppermute x0 -> x79, waiting for transfers between devices: none -> 260 us  [swap(): return lax.ppermute(value, axis, [(i, i ^ bit) for i in range(size)])]
    psum x4 -> x0, blocking collectives: 77.8 us -> none  [the longest x1 42.7 us: shards(): vectors = lax.psum(stacked, ('dp', 'mp'))]
    reduce_scatter x3 -> x0, waiting for transfers between devices: 66.4 us -> none  [the longest x1 34 us: shards(): lax.psum_scatter(contract_cols(deconv_grad, deconv_w).astype(jnp.bfloat16...]
    ppermute x0 -> x79, starting transfers between devices: none -> 58.9 us  [swap(): return lax.ppermute(value, axis, [(i, i ^ bit) for i in range(size)])]
    all_gather x2 -> x0, waiting for transfers between devices: 49.5 us -> none  [the longest x1 25.5 us: shards(): lax.all_gather(output_grad.astype(jnp.bfloat16), 'mp', axis=0, tiled=True)]
    dot_general x42 -> x33, matrix products: 105 us -> 65.1 us  [the longest x11 26.6 us: dot(): return jnp.dot(left, right, preferred_element_type=F32)]
    reduce_sum x16 -> x12, other arithmetic: 28.5 us -> 11.6 us  [the longest x1 3.12 us: shards(): jnp.sum(masked, axis=(1, 2))]
  transfers between devices with their start and end apart: 8 -> 79, of which waited for: 7 -> 44; matrix products, arithmetic and copies ran while one was open for 5% -> 23% of each run, Pallas kernels for 0% -> 3%
where the time goes in v1:
time: 514 us; the launch traced here: 504 us
  waiting for transfers between devices  260 us (51%)
  matrix products  65.1 us (13%)
  starting transfers between devices  58.9 us (11%)
  other arithmetic  52.7 us (10%)
  local copies, waits for them, and re-layouts  47.9 us (9%)
  Pallas kernels  16.9 us (3%)
    ppermute x79, waiting for transfers between devices, swap(): return lax.ppermute(value, axis, [(i, i ^ bit) for i in range(size)])  260 us
    ppermute x79, starting transfers between devices, swap(): return lax.ppermute(value, axis, [(i, i ^ bit) for i in range(size)])  58.9 us
    dot_general x11, matrix products, dot(): return jnp.dot(left, right, preferred_element_type=F32)  26.6 us
    dot_general x11, matrix products, dot_rows(): lax.dot_general(left, right, (((0,), (0,)), ((), ())), preferred_element_...  25 us
    unnamed x249, local copies, waits for them, and re-layouts  23 us
    dot_general x11, matrix products, dot_cols(): lax.dot_general(left, right, (((1,), (1,)), ((), ())), preferred_element_...  13.5 us
  transfers between devices with their start and end apart: 79, of which 44 were waited for; matrix products, arithmetic and copies ran while one was open for 23% of the time, Pallas kernels for 3%

profile of v1, /device:TPU:0, one launch (start us, length us, event | category | flops | bytes accessed | tf_op | source)
XLA Modules:
  0.0 504.2 jit_solution(6658884193422141923)
XLA Ops:
  17.9 7.4 %attend.1 = (bf16[1536,192]{1,0:T(8,128)(2,1)}, f32[3,8,512]{2,1,0:T(8,128)}) custom-call(s32[3]{0:T(128)} %len_ref.3, bf16[1536,576]{1,0:T(8,128)(2,1)} %add_convert_fusion.1.qkv_ref), custom_call_target="tpu_custom_call" | custom-call | flops 603979776 | bytes 2359296 | tf_op jit(solution)/shard_map/attend/pallas_call | solution.py:86
  66.2 4.4 multiply_convert_fusion.4
  72.3 16.0 %collective-permute-done.9 = bf16[768,768]{1,0:T(8,128)(2,1)S(1)} collective-permute-done((bf16[768,768]{1,0:T(8,128)(2,1)S(1)}, bf16[768,768]{1,0:T(8,128)(2,1)S(1)}, u32[]{:S(2)}, u32[]{:S(2)}) %collective-permute-start.9) | collective-permute-done | bytes 1179680 | tf_op jit(solution)/shard_map/ppermute | solution.py:32
  88.3 24.8 %collective-permute-done.11 = bf16[768,768]{1,0:T(8,128)(2,1)S(1)} collective-permute-done((bf16[768,768]{1,0:T(8,128)(2,1)S(1)}, bf16[768,768]{1,0:T(8,128)(2,1)S(1)}, u32[]{:S(2)}, u32[]{:S(2)}) %collective-permute-start.11) | collective-permute-done | bytes 1179680 | tf_op jit(solution)/shard_map/ppermute | solution.py:32
  113.2 4.6 multiply_convert_fusion.2
  118.6 4.5 multiply_convert_fusion.3
  124.3 4.4 multiply_convert_fusion.1
  204.6 9.5 %attend_back.1 = bf16[1536,576]{1,0:T(8,128)(2,1)} custom-call(s32[3]{0:T(128)} %len_ref.3, bf16[1536,576]{1,0:T(8,128)(2,1)} %add_convert_fusion.1.qkv_ref, bf16[1536,192]{1,0:T(8,128)(2,1)} %copy-done.53, f32[3,8,512]{2,1,0:T(8,128)} %get-tuple-element.23.lse_ref), custom_call_target="tpu_custom_call" | custom-call | flops 1509949440 | bytes 4128768 | tf_op jit(solution)/shard_map/attend_back/pallas_call | solution.py:147
  214.1 4.0 convolution_convert_fusion.4
  236.1 5.4 %collective-permute-done.24 = bf16[384,256]{1,0:T(8,128)(2,1)S(1)} collective-permute-done((bf16[384,256]{1,0:T(8,128)(2,1)}, bf16[384,256]{1,0:T(8,128)(2,1)S(1)}, u32[]{:S(2)}, u32[]{:S(2)}) %collective-permute-start.24) | collective-permute-done | bytes 196640 | tf_op jit(solution)/shard_map/ppermute | solution.py:32
  245.4 6.7 %collective-permute-done.25 = bf16[384,256]{1,0:T(8,128)(2,1)S(1)} collective-permute-done((bf16[384,256]{1,0:T(8,128)(2,1)S(1)}, bf16[384,256]{1,0:T(8,128)(2,1)S(1)}, u32[]{:S(2)}, u32[]{:S(2)}) %collective-permute-start.25) | collective-permute-done | bytes 196640 | tf_op jit(solution)/shard_map/ppermute | solution.py:32
  263.8 5.1 %collective-permute-done.45 = bf16[192,768]{1,0:T(8,128)(2,1)S(1)} collective-permute-done((bf16[192,768]{1,0:T(8,128)(2,1)S(1)}, bf16[192,768]{1,0:T(8,128)(2,1)S(1)}, u32[]{:S(2)}, u32[]{:S(2)}) %collective-permute-start.45) | collective-permute-done | bytes 294944 | tf_op jit(solution)/shard_map/ppermute | solution.py:32
  270.3 4.7 collective-permute-done.37
  282.6 7.2 %collective-permute-done.72 = bf16[768,256]{1,0:T(8,128)(2,1)S(1)} collective-permute-done((bf16[768,256]{1,0:T(8,128)(2,1)S(1)}, bf16[768,256]{1,0:T(8,128)(2,1)S(1)}, u32[]{:S(2)}, u32[]{:S(2)}) %collective-permute-start.72) | collective-permute-done | bytes 393248 | tf_op jit(solution)/shard_map/ppermute | solution.py:32
  295.0 7.1 %collective-permute-done.38 = bf16[192,576]{0,1:T(8,128)(2,1)S(1)} collective-permute-done((bf16[192,576]{0,1:T(8,128)(2,1)S(1)}, bf16[192,576]{0,1:T(8,128)(2,1)S(1)}, u32[]{:S(2)}, u32[]{:S(2)}) %collective-permute-start.38) | collective-permute-done | bytes 221216 | tf_op jit(solution)/shard_map/ppermute | solution.py:32
  314.1 4.6 collective-permute-done.39
  318.8 4.3 collective-permute-done.50
  324.3 4.4 collective-permute-done.73
  330.9 6.0 %collective-permute-done.40 = bf16[96,576]{0,1:T(8,128)(2,1)S(1)} collective-permute-done((bf16[96,576]{0,1:T(8,128)(2,1)S(1)}, bf16[96,576]{0,1:T(8,128)(2,1)S(1)}, u32[]{:S(2)}, u32[]{:S(2)}) %collective-permute-start.40) | collective-permute-done | bytes 110624 | tf_op jit(solution)/shard_map/ppermute | solution.py:32
  337.7 4.4 collective-permute-done.74
  348.7 4.0 collective-permute-done.75
  362.3 8.2 %collective-permute-done.41 = bf16[192,576]{0,1:T(8,128)(2,1)S(1)} collective-permute-done((bf16[192,576]{0,1:T(8,128)(2,1)S(1)}, bf16[192,576]{0,1:T(8,128)(2,1)S(1)}, u32[]{:S(2)}, u32[]{:S(2)}) %collective-permute-start.41) | collective-permute-done | bytes 221216 | tf_op jit(solution)/shard_map/ppermute | solution.py:32
  380.5 10.5 %collective-permute-done.78 = bf16[384,256]{1,0:T(8,128)(2,1)S(1)} collective-permute-done((bf16[384,256]{1,0:T(8,128)(2,1)S(1)}, bf16[384,256]{1,0:T(8,128)(2,1)S(1)}, u32[]{:S(2)}, u32[]{:S(2)}) %collective-permute-start.78) | collective-permute-done | bytes 196640 | tf_op jit(solution)/shard_map/ppermute | solution.py:32
  393.2 10.9 %collective-permute-done.63 = bf16[768,768]{1,0:T(8,128)(2,1)S(1)} collective-permute-done((bf16[768,768]{1,0:T(8,128)(2,1)S(1)}, bf16[768,768]{1,0:T(8,128)(2,1)S(1)}, u32[]{:S(2)}, u32[]{:S(2)}) %collective-permute-start.63) | collective-permute-done | bytes 1179680 | tf_op jit(solution)/shard_map/ppermute | solution.py:32
  405.6 21.3 %collective-permute-done.54 = bf16[768,768]{1,0:T(8,128)(2,1)S(1)} collective-permute-done((bf16[768,768]{1,0:T(8,128)(2,1)S(1)}, bf16[768,768]{1,0:T(8,128)(2,1)S(1)}, u32[]{:S(2)}, u32[]{:S(2)}) %collective-permute-start.54) | collective-permute-done | bytes 1179680 | tf_op jit(solution)/shard_map/ppermute | solution.py:32
  429.4 11.0 %collective-permute-done.55 = bf16[384,768]{1,0:T(8,128)(2,1)S(1)} collective-permute-done((bf16[384,768]{1,0:T(8,128)(2,1)S(1)}, bf16[384,768]{1,0:T(8,128)(2,1)S(1)}, u32[]{:S(2)}, u32[]{:S(2)}) %collective-permute-start.55) | collective-permute-done | bytes 589856 | tf_op jit(solution)/shard_map/ppermute | solution.py:32
  443.8 5.8 %collective-permute-done.56 = bf16[192,768]{1,0:T(8,128)(2,1)S(1)} collective-permute-done((bf16[192,768]{1,0:T(8,128)(2,1)S(1)}, bf16[192,768]{1,0:T(8,128)(2,1)S(1)}, u32[]{:S(2)}, u32[]{:S(2)}) %collective-permute-start.56) | collective-permute-done | bytes 294944 | tf_op jit(solution)/shard_map/ppermute | solution.py:32
  453.1 6.8 %collective-permute-done.57 = bf16[96,768]{1,0:T(8,128)(2,1)S(1)} collective-permute-done((bf16[96,768]{1,0:T(8,128)(2,1)S(1)}, bf16[96,768]{1,0:T(8,128)(2,1)S(1)}, u32[]{:S(2)}, u32[]{:S(2)}) %collective-permute-start.57) | collective-permute-done | bytes 147488 | tf_op jit(solution)/shard_map/ppermute | solution.py:32
  460.0 6.2 %collective-permute-done.67 = bf16[96,768]{1,0:T(8,128)(2,1)S(1)} collective-permute-done((bf16[96,768]{1,0:T(8,128)(2,1)S(1)}, bf16[96,768]{1,0:T(8,128)(2,1)S(1)}, u32[]{:S(2)}, u32[]{:S(2)}) %collective-permute-start.67) | collective-permute-done | bytes 147488 | tf_op jit(solution)/shard_map/ppermute | solution.py:32
  469.3 7.0 %collective-permute-done.68 = bf16[192,768]{1,0:T(8,128)(2,1)S(1)} collective-permute-done((bf16[192,768]{1,0:T(8,128)(2,1)S(1)}, bf16[192,768]{1,0:T(8,128)(2,1)S(1)}, u32[]{:S(2)}, u32[]{:S(2)}) %collective-permute-start.68) | collective-permute-done | bytes 294944 | tf_op jit(solution)/shard_map/ppermute | solution.py:32
  484.1 8.6 %collective-permute-done.69 = bf16[384,768]{1,0:T(8,128)(2,1)S(1)} collective-permute-done((bf16[384,768]{1,0:T(8,128)(2,1)S(1)}, bf16[384,768]{1,0:T(8,128)(2,1)S(1)}, u32[]{:S(2)}, u32[]{:S(2)}) %collective-permute-start.69) | collective-permute-done | bytes 589856 | tf_op jit(solution)/shard_map/ppermute | solution.py:32
  494.6 7.4 %collective-permute-done.60 = bf16[384,768]{1,0:T(8,128)(2,1)S(1)} collective-permute-done((bf16[384,768]{1,0:T(8,128)(2,1)S(1)}, bf16[384,768]{1,0:T(8,128)(2,1)S(1)}, u32[]{:S(2)}, u32[]{:S(2)}) %collective-permute-start.60) | collective-permute-done | bytes 589856 | tf_op jit(solution)/shard_map/ppermute | solution.py:32
  (589 shorter events, 254.0 us)
Async XLA Ops:
  0.7 48.9 %collective-permute-start.4 = (bf16[192,768]{1,0:T(8,128)(2,1)}, bf16[192,768]{1,0:T(8,128)(2,1)}, u32[]{:S(2)}, u32[]{:S(2)}) collective-permute-start(bf16[192,768]{1,0:T(8,128)(2,1)} %param.30), channel_id=1, source_target_pairs={{0,2},{1,3},{2,0},{3,1},{4,6},{5,7},{6,4},{7,5},{8,10},{9,11},{10,... | collective-permute-start | bytes 884744 | tf_op jit(solution)/shard_map/ppermute | solution.py:32
  3.7 46.0 %collective-permute-start.3 = (bf16[192,768]{1,0:T(8,128)(2,1)}, bf16[192,768]{1,0:T(8,128)(2,1)}, u32[]{:S(2)}, u32[]{:S(2)}) collective-permute-start(bf16[192,768]{1,0:T(8,128)(2,1)} %param.30), channel_id=1, source_target_pairs={{0,1},{1,0},{2,3},{3,2},{4,5},{5,4},{6,7},{7,6},{8,9},{9,8},{10,11... | collective-permute-start | bytes 884744 | tf_op jit(solution)/shard_map/ppermute | solution.py:32
  5.0 29.1 %collective-permute-start.10 = (bf16[1,768]{1,0:T(2,128)(2,1)}, bf16[1,768]{1,0:T(2,128)(2,1)}, u32[]{:S(2)}, u32[]{:S(2)}) collective-permute-start(bf16[1,768]{1,0:T(2,128)(2,1)} %reshape.587), channel_id=1, source_target_pairs={{0,2},{1,3},{2,0},{3,1},{4,6},{5,7},{6,4},{7,5},{8,10},{9,11},{10,... | collective-permute-start | bytes 4616 | tf_op jit(solution)/shard_map/ppermute | solution.py:32
  5.1 30.9 %collective-permute-start.7 = (bf16[1,768]{1,0:T(2,128)(2,1)}, bf16[1,768]{1,0:T(2,128)(2,1)}, u32[]{:S(2)}, u32[]{:S(2)}) collective-permute-start(bf16[1,768]{1,0:T(2,128)(2,1)} %reshape.587), channel_id=1, source_target_pairs={{0,1},{1,0},{2,3},{3,2},{4,5},{5,4},{6,7},{7,6},{8,9},{9,8},{10,11... | collective-permute-start | bytes 4616 | tf_op jit(solution)/shard_map/ppermute | solution.py:32
  7.6 30.2 %collective-permute-start.18 = (bf16[384,256]{1,0:T(8,128)(2,1)}, bf16[384,256]{1,0:T(8,128)(2,1)}, u32[]{:S(2)}, u32[]{:S(2)}) collective-permute-start(bf16[384,256]{1,0:T(8,128)(2,1)} %get-tuple-element.86), channel_id=1, source_target_pairs={{0,1},{1,0},{2,3},{3,2},{4,5},{5,4},{6,7},{7,6},{8,9},{9,8},{10,11... | collective-permute-start | bytes 589832 | tf_op jit(solution)/shard_map/ppermute | solution.py:32
  37.3 14.8 %collective-permute-start.15 = (bf16[768,256]{1,0:T(8,128)(2,1)}, bf16[768,256]{1,0:T(8,128)(2,1)}, u32[]{:S(2)}, u32[]{:S(2)}) collective-permute-start(bf16[768,256]{1,0:T(8,128)(2,1)} %param.38), channel_id=1, source_target_pairs={{0,1},{1,0},{2,3},{3,2},{4,5},{5,4},{6,7},{7,6},{8,9},{9,8},{10,11... | collective-permute-start | bytes 1179656 | tf_op jit(solution)/shard_map/ppermute | solution.py:32
  42.1 13.5 %collective-permute-start.16 = (bf16[768,256]{1,0:T(8,128)(2,1)}, bf16[768,256]{1,0:T(8,128)(2,1)}, u32[]{:S(2)}, u32[]{:S(2)}) collective-permute-start(bf16[768,256]{1,0:T(8,128)(2,1)} %param.38), channel_id=1, source_target_pairs={{0,2},{1,3},{2,0},{3,1},{4,6},{5,7},{6,4},{7,5},{8,10},{9,11},{10,... | collective-permute-start | bytes 1179656 | tf_op jit(solution)/shard_map/ppermute | solution.py:32
  55.6 32.7 %collective-permute-start.9 = (bf16[768,768]{1,0:T(8,128)(2,1)S(1)}, bf16[768,768]{1,0:T(8,128)(2,1)S(1)}, u32[]{:S(2)}, u32[]{:S(2)}) collective-permute-start(bf16[768,768]{1,0:T(8,128)(2,1)S(1)} %copy-done.39), channel_id=1, source_target_pairs={{0,2},{1,3},{2,0},{3,1},{4,6},{5,7},{6,4},{7,5},{8,10},{9,11},{10,... | collective-permute-start | bytes 3538952 | tf_op jit(solution)/shard_map/ppermute | solution.py:32
  58.4 60.1 %collective-permute-start.6 = (bf16[768,768]{1,0:T(8,128)(2,1)S(1)}, bf16[768,768]{1,0:T(8,128)(2,1)S(1)}, u32[]{:S(2)}, u32[]{:S(2)}) collective-permute-start(bf16[768,768]{1,0:T(8,128)(2,1)S(1)} %copy-done.39), channel_id=1, source_target_pairs={{0,1},{1,0},{2,3},{3,2},{4,5},{5,4},{6,7},{7,6},{8,9},{9,8},{10,11... | collective-permute-start | bytes 3538952 | tf_op jit(solution)/shard_map/ppermute | solution.py:32
  58.5 54.7 %collective-permute-start.11 = (bf16[768,768]{1,0:T(8,128)(2,1)S(1)}, bf16[768,768]{1,0:T(8,128)(2,1)S(1)}, u32[]{:S(2)}, u32[]{:S(2)}) collective-permute-start(bf16[768,768]{1,0:T(8,128)(2,1)S(1)} %copy-done.37), channel_id=1, source_target_pairs={{0,2},{1,3},{2,0},{3,1},{4,6},{5,7},{6,4},{7,5},{8,10},{9,11},{10,... | collective-permute-start | bytes 3538952 | tf_op jit(solution)/shard_map/ppermute | solution.py:32
  59.5 63.5 %collective-permute-start.8 = (bf16[768,768]{1,0:T(8,128)(2,1)S(1)}, bf16[768,768]{1,0:T(8,128)(2,1)S(1)}, u32[]{:S(2)}, u32[]{:S(2)}) collective-permute-start(bf16[768,768]{1,0:T(8,128)(2,1)S(1)} %copy-done.37), channel_id=1, source_target_pairs={{0,1},{1,0},{2,3},{3,2},{4,5},{5,4},{6,7},{7,6},{8,9},{9,8},{10,11... | collective-permute-start | bytes 3538952 | tf_op jit(solution)/shard_map/ppermute | solution.py:32
  88.3 35.9 %collective-permute-start.12 = (bf16[768,768]{1,0:T(8,128)(2,1)S(1)}, bf16[768,768]{1,0:T(8,128)(2,1)S(1)}, u32[]{:S(2)}, u32[]{:S(2)}) collective-permute-start(bf16[768,768]{1,0:T(8,128)(2,1)S(1)} %collective-permute-done.9), channel_id=1, source_target_pairs={{0,1},{1,0},{2,3},{3,2},{4,5},{5,4},{6,7},{7,6},{8,9},{9,8},{10,11... | collective-permute-start | bytes 3538952 | tf_op jit(solution)/shard_map/ppermute | solution.py:32
  113.2 15.6 %collective-permute-start.14 = (bf16[768,768]{1,0:T(8,128)(2,1)S(1)}, bf16[768,768]{1,0:T(8,128)(2,1)S(1)}, u32[]{:S(2)}, u32[]{:S(2)}) collective-permute-start(bf16[768,768]{1,0:T(8,128)(2,1)S(1)} %collective-permute-done.11), channel_id=1, source_target_pairs={{0,1},{1,0},{2,3},{3,2},{4,5},{5,4},{6,7},{7,6},{8,9},{9,8},{10,11... | collective-permute-start | bytes 3538952 | tf_op jit(solution)/shard_map/ppermute | solution.py:32
  172.5 88.7 %collective-permute-start.71 = (bf16[768,256]{1,0:T(8,128)(2,1)}, bf16[768,256]{1,0:T(8,128)(2,1)}, u32[]{:S(2)}, u32[]{:S(2)}) collective-permute-start(bf16[768,256]{1,0:T(8,128)(2,1)} %get-tuple-element.70), channel_id=1, source_target_pairs={{0,1},{1,0},{2,3},{3,2},{4,5},{5,4},{6,7},{7,6},{8,9},{9,8},{10,11... | collective-permute-start | bytes 1179656 | tf_op jit(solution)/shard_map/ppermute | solution.py:32
  172.5 109.1 %collective-permute-start.70 = (bf16[768,256]{1,0:T(8,128)(2,1)}, bf16[768,256]{1,0:T(8,128)(2,1)}, u32[]{:S(2)}, u32[]{:S(2)}) collective-permute-start(bf16[768,256]{1,0:T(8,128)(2,1)} %get-tuple-element.69), channel_id=1, source_target_pairs={{0,1},{1,0},{2,3},{3,2},{4,5},{5,4},{6,7},{7,6},{8,9},{9,8},{10,11... | collective-permute-start | bytes 1179656 | tf_op jit(solution)/shard_map/ppermute | solution.py:32
  173.0 185.2 %collective-permute-start.62 = (bf16[768,768]{1,0:T(8,128)(2,1)}, bf16[768,768]{1,0:T(8,128)(2,1)}, u32[]{:S(2)}, u32[]{:S(2)}) collective-permute-start(bf16[768,768]{1,0:T(8,128)(2,1)} %convolution_convert_fusion), channel_id=1, source_target_pairs={{0,1},{1,0},{2,3},{3,2},{4,5},{5,4},{6,7},{7,6},{8,9},{9,8},{10,11... | collective-permute-start | bytes 3538952 | tf_op jit(solution)/shard_map/ppermute | solution.py:32
  200.7 57.4 %collective-permute-start.44 = (bf16[192,768]{1,0:T(8,128)(2,1)}, bf16[192,768]{1,0:T(8,128)(2,1)}, u32[]{:S(2)}, u32[]{:S(2)}) collective-permute-start(bf16[192,768]{1,0:T(8,128)(2,1)} %get-tuple-element.76), channel_id=1, source_target_pairs={{0,1},{1,0},{2,3},{3,2},{4,5},{5,4},{6,7},{7,6},{8,9},{9,8},{10,11... | collective-permute-start | bytes 884744 | tf_op jit(solution)/shard_map/ppermute | solution.py:32
  261.1 132.1 %collective-permute-start.61 = (bf16[768,768]{1,0:T(8,128)(2,1)}, bf16[768,768]{1,0:T(8,128)(2,1)S(1)}, u32[]{:S(2)}, u32[]{:S(2)}) collective-permute-start(bf16[768,768]{1,0:T(8,128)(2,1)} %convolution_convert_fusion.1), channel_id=1, source_target_pairs={{0,1},{1,0},{2,3},{3,2},{4,5},{5,4},{6,7},{7,6},{8,9},{9,8},{10,11... | collective-permute-start | bytes 3538952 | tf_op jit(solution)/shard_map/ppermute | solution.py:32
  262.6 12.4 %collective-permute-start.37 = (bf16[384,576]{0,1:T(8,128)(2,1)S(1)}, bf16[384,576]{0,1:T(8,128)(2,1)S(1)}, u32[]{:S(2)}, u32[]{:S(2)}) collective-permute-start(bf16[384,576]{0,1:T(8,128)(2,1)S(1)} %copy-done.60), channel_id=1, source_target_pairs={{0,4},{4,0},{8,12},{12,8},{16,20},{20,16},{24,28},{28,24},{1,5},{5... | collective-permute-start | bytes 1327112 | tf_op jit(solution)/shard_map/ppermute | solution.py:32
  281.4 80.0 %collective-permute-start.53 = (bf16[768,768]{1,0:T(8,128)(2,1)S(1)}, bf16[768,768]{1,0:T(8,128)(2,1)S(1)}, u32[]{:S(2)}, u32[]{:S(2)}) collective-permute-start(bf16[768,768]{1,0:T(8,128)(2,1)S(1)} %copy-done.108), channel_id=1, source_target_pairs={{0,1},{1,0},{2,3},{3,2},{4,5},{5,4},{6,7},{7,6},{8,9},{9,8},{10,11... | collective-permute-start | bytes 3538952 | tf_op jit(solution)/shard_map/ppermute | solution.py:32
  282.6 123.0 %collective-permute-start.52 = (bf16[768,768]{1,0:T(8,128)(2,1)S(1)}, bf16[768,768]{1,0:T(8,128)(2,1)S(1)}, u32[]{:S(2)}, u32[]{:S(2)}) collective-permute-start(bf16[768,768]{1,0:T(8,128)(2,1)S(1)} %copy-done.107), channel_id=1, source_target_pairs={{0,1},{1,0},{2,3},{3,2},{4,5},{5,4},{6,7},{7,6},{8,9},{9,8},{10,11... | collective-permute-start | bytes 3538952 | tf_op jit(solution)/shard_map/ppermute | solution.py:32
  358.1 18.2 %collective-permute-start.29 = (bf16[384,768]{1,0:T(8,128)(2,1)S(1)}, bf16[384,768]{1,0:T(8,128)(2,1)S(1)}, u32[]{:S(2)}, u32[]{:S(2)}) collective-permute-start(bf16[384,768]{1,0:T(8,128)(2,1)S(1)} %copy-done.56), channel_id=1, source_target_pairs={{0,1},{1,0},{2,3},{3,2},{4,5},{5,4},{6,7},{7,6},{8,9},{9,8},{10,11... | collective-permute-start | bytes 1769480 | tf_op jit(solution)/shard_map/ppermute | solution.py:32
  358.2 19.1 %collective-permute-start.31 = (bf16[384,768]{1,0:T(8,128)(2,1)S(1)}, bf16[384,768]{1,0:T(8,128)(2,1)S(1)}, u32[]{:S(2)}, u32[]{:S(2)}) collective-permute-start(bf16[384,768]{1,0:T(8,128)(2,1)S(1)} %add_convert_fusion.8), channel_id=1, source_target_pairs={{0,2},{1,3},{2,0},{3,1},{4,6},{5,7},{6,4},{7,5},{8,10},{9,11},{10,... | collective-permute-start | bytes 1769480 | tf_op jit(solution)/shard_map/ppermute | solution.py:32
  375.2 28.9 %collective-permute-start.63 = (bf16[768,768]{1,0:T(8,128)(2,1)S(1)}, bf16[768,768]{1,0:T(8,128)(2,1)S(1)}, u32[]{:S(2)}, u32[]{:S(2)}) collective-permute-start(bf16[768,768]{1,0:T(8,128)(2,1)S(1)} %add_convert_fusion.3), channel_id=1, source_target_pairs={{0,2},{1,3},{2,0},{3,1},{4,6},{5,7},{6,4},{7,5},{8,10},{9,11},{10,... | collective-permute-start | bytes 3538952 | tf_op jit(solution)/shard_map/ppermute | solution.py:32
  376.3 16.6 %collective-permute-start.42 = (bf16[384,576]{0,1:T(8,128)(2,1)S(1)}, bf16[384,576]{0,1:T(8,128)(2,1)S(1)}, u32[]{:S(2)}, u32[]{:S(2)}) collective-permute-start(bf16[384,576]{0,1:T(8,128)(2,1)S(1)} %pad_maximum_fusion.4), channel_id=1, source_target_pairs={{0,4},{4,0},{8,12},{12,8},{16,20},{20,16},{24,28},{28,24},{1,5},{5... | collective-permute-start | bytes 1327112 | tf_op jit(solution)/shard_map/ppermute | solution.py:32
  377.4 13.6 %collective-permute-start.78 = (bf16[384,256]{1,0:T(8,128)(2,1)S(1)}, bf16[384,256]{1,0:T(8,128)(2,1)S(1)}, u32[]{:S(2)}, u32[]{:S(2)}) collective-permute-start(bf16[384,256]{1,0:T(8,128)(2,1)S(1)} %pad_maximum_fusion.8), channel_id=1, source_target_pairs={{0,4},{4,0},{8,12},{12,8},{16,20},{20,16},{24,28},{28,24},{1,5},{5... | collective-permute-start | bytes 589832 | tf_op jit(solution)/shard_map/ppermute | solution.py:32
  390.9 36.0 %collective-permute-start.54 = (bf16[768,768]{1,0:T(8,128)(2,1)S(1)}, bf16[768,768]{1,0:T(8,128)(2,1)S(1)}, u32[]{:S(2)}, u32[]{:S(2)}) collective-permute-start(bf16[768,768]{1,0:T(8,128)(2,1)S(1)} %add_convert_fusion.5), channel_id=1, source_target_pairs={{0,2},{1,3},{2,0},{3,1},{4,6},{5,7},{6,4},{7,5},{8,10},{9,11},{10,... | collective-permute-start | bytes 3538952 | tf_op jit(solution)/shard_map/ppermute | solution.py:32
  404.6 24.0 %collective-permute-start.64 = (bf16[384,768]{1,0:T(8,128)(2,1)S(1)}, bf16[384,768]{1,0:T(8,128)(2,1)S(1)}, u32[]{:S(2)}, u32[]{:S(2)}) collective-permute-start(bf16[384,768]{1,0:T(8,128)(2,1)S(1)} %broadcast_select_fusion.2), channel_id=1, source_target_pairs={{0,4},{4,0},{8,12},{12,8},{16,20},{20,16},{24,28},{28,24},{1,5},{5... | collective-permute-start | bytes 1769480 | tf_op jit(solution)/shard_map/ppermute | solution.py:32
  427.4 12.9 %collective-permute-start.55 = (bf16[384,768]{1,0:T(8,128)(2,1)S(1)}, bf16[384,768]{1,0:T(8,128)(2,1)S(1)}, u32[]{:S(2)}, u32[]{:S(2)}) collective-permute-start(bf16[384,768]{1,0:T(8,128)(2,1)S(1)} %broadcast_select_fusion.5), channel_id=1, source_target_pairs={{0,4},{4,0},{8,12},{12,8},{16,20},{20,16},{24,28},{28,24},{1,5},{5... | collective-permute-start | bytes 1769480 | tf_op jit(solution)/shard_map/ppermute | solution.py:32
  450.2 16.0 %collective-permute-start.67 = (bf16[96,768]{1,0:T(8,128)(2,1)S(1)}, bf16[96,768]{1,0:T(8,128)(2,1)S(1)}, u32[]{:S(2)}, u32[]{:S(2)}) collective-permute-start(bf16[96,768]{1,0:T(8,128)(2,1)S(1)} %add_convert_fusion.19), channel_id=1, source_target_pairs={{0,16},{4,20},{8,24},{12,28},{16,0},{20,4},{24,8},{28,12},{1,17},{... | collective-permute-start | bytes 442376 | tf_op jit(solution)/shard_map/ppermute | solution.py:32
  476.5 16.3 %collective-permute-start.69 = (bf16[384,768]{1,0:T(8,128)(2,1)S(1)}, bf16[384,768]{1,0:T(8,128)(2,1)S(1)}, u32[]{:S(2)}, u32[]{:S(2)}) collective-permute-start(bf16[384,768]{1,0:T(8,128)(2,1)S(1)} %pad_maximum_fusion.3), channel_id=1, source_target_pairs={{0,4},{4,0},{8,12},{12,8},{16,20},{20,16},{24,28},{28,24},{1,5},{5... | collective-permute-start | bytes 1769480 | tf_op jit(solution)/shard_map/ppermute | solution.py:32
  481.5 20.5 %collective-permute-start.60 = (bf16[384,768]{1,0:T(8,128)(2,1)S(1)}, bf16[384,768]{1,0:T(8,128)(2,1)S(1)}, u32[]{:S(2)}, u32[]{:S(2)}) collective-permute-start(bf16[384,768]{1,0:T(8,128)(2,1)S(1)} %pad_maximum_fusion.2), channel_id=1, source_target_pairs={{0,4},{4,0},{8,12},{12,8},{16,20},{20,16},{24,28},{28,24},{1,5},{5... | collective-permute-start | bytes 1769480 | tf_op jit(solution)/shard_map/ppermute | solution.py:32
  (167 other events, 945.4 us)
